TPU v7x, 512 devices: a whole 4x8x8 slice. The times are simulated.
512 devices in a mesh: dp: 4 (over x), ep: 128 (over z, y, core).
Axes of the slice: x: 4, y: 8, z: 8, core: 2. Of those that a mesh axis runs over, the one named last changes fastest.
Arguments:
- tokens: bfloat16 [128, 16, 2048], P('ep', 'dp'), may hold values from -6 to 6
- dest_ids: int32 [128, 16, 8], P('ep', 'dp'), may hold values from 0 to 127, all different within a row; in each aligned block of 16 rows (0 to 15, 16 to 31, ..., all dimensions but the last counted through in order) at most 2 rows name the same one
- gate_fixed: int32 [128, 16, 8], P('ep', 'dp'), may hold values from 1 to 65535
- gate_up: bfloat16 [128, 2, 768, 2048], P('ep', None, 'dp'), may hold values from -0.125 to 0.125
- down: bfloat16 [128, 768, 2048], P('ep', 'dp'), may hold values from -0.21875 to 0.21875
Outputs:
- mixed: bfloat16 [128, 16, 2048], P('ep', 'dp')
Inputs may be any that keep to these rules, and one draw needn't show every extreme that they name: `dest_ids`: each row names 8 different experts; within one column's 16 rows no expert is named by more than 2 routes.
All inputs are finite; a program needn't handle non-finite values.
Results may differ from a plain program's by a relative error of at most 0.012.
Values may be sent and summed in bfloat16 or wider, within the bound.
A program may use at most 192 MiB of HBM per device.

v0:
```python
import jax
import jax.numpy as jnp
from jax import lax
from jax.sharding import PartitionSpec as P


def feed_forward(rows, pair, lower):
    gate = jnp.einsum("nd,hd->nh", rows, pair[0], preferred_element_type=jnp.float32)
    upper = jnp.einsum("nd,hd->nh", rows, pair[1], preferred_element_type=jnp.float32)
    hidden = (jax.nn.silu(gate) * upper).astype(jnp.bfloat16)
    return jnp.dot(hidden, lower, preferred_element_type=jnp.float32).astype(jnp.bfloat16)


def per_device(tokens, dest_ids, gate_fixed, gate_up, down):
    peer_count = lax.axis_size("ep")
    own_rows = tokens[0]
    width = own_rows.shape[1]
    top_count = dest_ids.shape[2]
    route_table = jnp.concatenate([dest_ids[0], gate_fixed[0]], axis=1)
    column_table = lax.all_gather(route_table, "dp", axis=0, tiled=True)
    col_rows = column_table.shape[0]
    capacity = min(col_rows, max(2, 2 * col_rows * top_count // peer_count))
    target_dev = column_table[:, :top_count].reshape(-1)
    gate_raw = column_table[:, top_count:].astype(jnp.float32)
    gate_norm = gate_raw / jnp.sum(gate_raw, axis=1, keepdims=True)
    marks = (target_dev[:, None] == jnp.arange(peer_count, dtype=jnp.int32)[None, :]).astype(
        jnp.int32
    )
    slot_rank = jnp.sum(jnp.cumsum(marks, axis=0) * marks, axis=1) - 1
    slot_index = target_dev * capacity + slot_rank
    source_row = jnp.arange(target_dev.shape[0], dtype=jnp.int32) // top_count
    column_rows = lax.all_gather(own_rows, "dp", axis=0, tiled=True)
    send_block = (
        jnp.zeros((peer_count * capacity, width), jnp.bfloat16)
        .at[slot_index]
        .set(column_rows[source_row])
        .reshape(peer_count, capacity, width)
    )
    rows = lax.all_to_all(send_block, "ep", split_axis=0, concat_axis=0, tiled=True)
    flat_rows = rows.reshape(-1, rows.shape[2])
    own_out = feed_forward(flat_rows, gate_up[0], down[0])
    returned = lax.all_to_all(
        own_out.reshape(rows.shape[0], rows.shape[1], -1),
        "ep",
        split_axis=0,
        concat_axis=0,
        tiled=True,
    )
    flat_back = returned.reshape(peer_count * capacity, -1)
    weighted = flat_back[slot_index].astype(jnp.float32) * gate_norm.reshape(-1)[:, None]
    summed = jnp.sum(weighted.reshape(col_rows, top_count, -1), axis=1)
    mine = lax.psum_scatter(summed.astype(jnp.bfloat16), "dp", scatter_dimension=0, tiled=True)
    return mine[None]


def solution(mesh):
    return jax.shard_map(
        per_device,
        mesh=mesh,
        in_specs=(
            P("ep", "dp", None),
            P("ep", "dp", None),
            P("ep", "dp", None),
            P("ep", None, "dp", None),
            P("ep", "dp", None),
        ),
        out_specs=P("ep", "dp", None),
        check_vma=False,
    )
```

profile of v0, /device:TPU:8, one launch (start us, length us, event | category | flops | bytes accessed | tf_op | source)
XLA Modules:
  0.0 182.8 jit_solution(7191116500669155721)
XLA Ops:
  6.5 0.0 copy-start
  6.5 0.8 add_bitcast_fusion
  7.4 11.1 %all-gather.1 = s32[4,4,16]{2,1,0:T(4,128)S(1)} all-gather(s32[1,4,16]{2,1,0:T(4,128)S(1)} %add_bitcast_fusion), channel_id=1, replica_groups=mesh['dp'=4,'ep'=128] {'dp'}, dimensions={0}, use_global_device_ids=true | all-gather | bytes 1280 | tf_op jit(solution)/shard_map/all_gather | solution.py:20
  18.5 0.1 eq.15
  18.6 0.1 fusion.19
  18.7 0.2 reduce_window_sum.11
  18.9 0.2 select_reduce_fusion
  19.1 0.1 mul.37
  19.2 0.7 copy.7
  19.9 12.0 %all-gather = bf16[1,16,2048]{2,0,1:T(2,128)(2,1)S(1)} all-gather(bf16[1,4,2048]{2,0,1:T(2,128)(2,1)S(1)} %copy.7), channel_id=2, replica_groups=mesh['dp'=4,'ep'=128] {'dp'}, dimensions={1}, use_global_device_ids=true | all-gather | bytes 81920 | tf_op jit(solution)/shard_map/all_gather | solution.py:32
  32.0 3.4 %scatter_custom_fusion = bf16[256,2048]{1,0:T(8,128)(2,1)S(1)} fusion(s32[128]{0:T(128)S(1)} %fusion.23, bf16[16,2048]{1,0:T(8,128)(2,1)S(1)} %bitcast.37, s32[1024]{0:T(1024)S(1)} %pad_clamp_fusion.1, bf16[]{:T(256)} %constant.28.clone.1), kind=kCustom, calls=%fused_computation.14 | custom fusion | bytes 1048578 | tf_op jit(solution)/shard_map/scatter | solution.py:36
  35.4 0.7 reshape.105
  36.1 48.6 %all_to_all.10 = bf16[128,2,2048]{2,1,0:T(2,128)(2,1)S(1)} all-to-all(bf16[128,2,2048]{2,1,0:T(2,128)(2,1)S(1)} %reshape.105), channel_id=1, replica_groups=mesh['dp'=4,'ep'=128] {'ep'}, dimensions={0} | all-to-all | bytes 2097152 | tf_op jit(solution)/shard_map/all_to_all | solution.py:39
  84.7 0.4 reshape.106
  85.1 1.6 fusion.5
  86.8 0.0 copy-done
  86.8 2.6 %convolution_convert_fusion = bf16[256,2048]{1,0:T(8,128)(2,1)S(1)} fusion(bf16[256,2048]{1,0:T(8,128)(2,1)S(1)} %reshape.106, bf16[1,192,2048]{2,1,0:T(8,128)(2,1)S(1)} %copy-done, bf16[1,2,192,2048]{3,2,1,0:T(8,128)(2,1)} %param.8, f32[256,192]{0,1:T(8,128)S(1)} %fusion.5), kind=kOutput, calls=%fused_computation.3 | convolution fusion | flops 403472384 | bytes 3866624 | tf_op jit(solution)/shard_map/dot_general | solution.py:11
  89.3 1.5 reshape.107
  90.9 5.9 %all-to-all-start.1 = ((bf16[128,2,2048]{2,1,0:T(2,128)(2,1)}), bf16[128,2,2048]{2,1,0:T(2,128)(2,1)S(1)}, u32[]{:S(2)}, u32[]{:S(2)}) async-start(bf16[128,2,2048]{2,1,0:T(2,128)(2,1)} %reshape.107), calls=%async_computation.1 | async-start | bytes 2097152 | tf_op jit(solution)/shard_map/all_to_all | solution.py:42
  96.8 0.0 all-reduce.3.cloned.1.call-start
  96.9 0.2 fusion.21
  97.0 0.1 fusion.20
  97.1 31.1 %all-to-all-done.1 = bf16[128,2,2048]{2,1,0:T(2,128)(2,1)S(1)} async-done(((bf16[128,2,2048]{2,1,0:T(2,128)(2,1)}), bf16[128,2,2048]{2,1,0:T(2,128)(2,1)S(1)}, u32[]{:S(2)}, u32[]{:S(2)}) %all-to-all-start.1) | async-done | bytes 1048608 | tf_op jit(solution)/shard_map/all_to_all | solution.py:42
  128.2 0.4 reshape.108
  128.7 0.9 gather_fusion
  129.6 1.1 fusion.1
  130.7 0.0 all-reduce.3.cloned.1.call-update
  130.7 1.3 dynamic-slice
  132.6 42.0 %all-reduce.3.cloned.1.call-done = bf16[16,2048]{1,0:T(8,128)(2,1)} async-done(((bf16[16,2048]{1,0:T(8,128)(2,1)}), bf16[16,2048]{1,0:T(8,128)(2,1)}) %all-reduce.3.cloned.1.call-update) | async-done | bytes 65552
  174.6 1.4 dynamic-slice_bitcast_fusion
  (6 shorter events, 0.1 us)
Async XLA Ops:
  6.5 80.2 %copy-start = (bf16[1,192,2048]{2,1,0:T(8,128)(2,1)S(1)}, bf16[1,192,2048]{2,1,0:T(8,128)(2,1)}, u32[]{:S(2)}) copy-start(bf16[1,192,2048]{2,1,0:T(8,128)(2,1)} %param.9) | copy-start | bytes 2359300
  90.9 37.4 %all-to-all-start.1 = ((bf16[128,2,2048]{2,1,0:T(2,128)(2,1)}), bf16[128,2,2048]{2,1,0:T(2,128)(2,1)S(1)}, u32[]{:S(2)}, u32[]{:S(2)}) async-start(bf16[128,2,2048]{2,1,0:T(2,128)(2,1)} %reshape.107), calls=%async_computation.1 | async-start | bytes 2097152 | tf_op jit(solution)/shard_map/all_to_all | solution.py:42
  96.8 77.8 %all-reduce.3.cloned.1.call-start = ((), (), s32[]{:S(2)}) async-start(), calls=%async_computation.2 | async-start | bytes 131072
Sparse Core Ops, SparseCore 0:
  130.8 43.7 all-reduce.2
where the time goes:
time: 183 us
  waiting for transfers between devices  73.1 us (40%)
  blocking collectives  71.7 us (39%)
  between operations  14.2 us (8%)
  local copies, waits for them, and re-layouts  11 us (6%)
  starting transfers between devices  5.97 us (3%)
  matrix products  4.21 us (2%)
  other arithmetic  2.64 us (1%)
    all_to_all x1, blocking collectives, per_device(): lax.all_to_all(send_block, 'ep', split_axis=0, concat_axis=0, tiled=True)  48.6 us
    unnamed x2, waiting for transfers between devices  42 us
    all_to_all x1, waiting for transfers between devices, per_device(): lax.all_to_all(own_out.reshape(rows.shape[0], rows.shape[1], -1), 'ep', s...  31.1 us
    all_gather x1, blocking collectives, per_device(): column_rows = lax.all_gather(own_rows, 'dp', axis=0, tiled=True)  12 us
    all_gather x1, blocking collectives, per_device(): column_table = lax.all_gather(route_table, 'dp', axis=0, tiled=True)  11.1 us
    all_to_all x1, starting transfers between devices, per_device(): lax.all_to_all(own_out.reshape(rows.shape[0], rows.shape[1], -1), 'ep', s...  5.93 us
  transfers between devices with their start and end apart: 2, of which 2 were waited for; matrix products, arithmetic and copies ran while one was open for 1% of the time, Pallas kernels for 0%

commit v1 on v0

--- a/solution.py
+++ b/solution.py
@@ -2,6 +2,15 @@
 import jax.numpy as jnp
 from jax import lax
 from jax.sharding import PartitionSpec as P
+
+
+def define_the_counts(array_in, which_dim):
+    array_in = jnp.moveaxis(array_in, 0, which_dim)
+    a_now = array_in.shape
+    frame_out = array_in.reshape(
+        *a_now[:which_dim], a_now[which_dim] * a_now[which_dim + 1], *a_now[which_dim + 2 :]
+    )
+    return frame_out
 
 
 def feed_forward(rows, pair, lower):
@@ -12,6 +21,25 @@
 
 
 def per_device(tokens, dest_ids, gate_fixed, gate_up, down):
+
+    def keep_up_copies_now(shard_in, net_axis, out_dim):
+        n_all = lax.axis_size(net_axis)
+        ledger = tuple(((idx, (idx + 1) % n_all) for idx in range(n_all)))
+        n_now, v1 = ([], [])
+        k0 = 0
+        seen = tuple(((h, no) for no, h in ledger))
+        while k0 < n_all - 1:
+            if k0 % 2 == 0:
+                n_now.append(lax.ppermute(n_now[-1] if n_now else shard_in, net_axis, ledger))
+            else:
+                v1.append(lax.ppermute(v1[-1] if v1 else shard_in, net_axis, seen))
+            k0 += 1
+        even = jnp.stack([*n_now[::-1], shard_in, *v1])
+        ready = lax.axis_index(net_axis) - len(n_now)
+        even = even[(jnp.arange(n_all) - ready) % n_all]
+        part_next = define_the_counts(even, out_dim)
+        return part_next
+
     peer_count = lax.axis_size("ep")
     own_rows = tokens[0]
     width = own_rows.shape[1]
@@ -29,7 +57,7 @@
     slot_rank = jnp.sum(jnp.cumsum(marks, axis=0) * marks, axis=1) - 1
     slot_index = target_dev * capacity + slot_rank
     source_row = jnp.arange(target_dev.shape[0], dtype=jnp.int32) // top_count
-    column_rows = lax.all_gather(own_rows, "dp", axis=0, tiled=True)
+    column_rows = keep_up_copies_now(own_rows, "dp", 0)
     send_block = (
         jnp.zeros((peer_count * capacity, width), jnp.bfloat16)
         .at[slot_index]

time: 183 us -> 185 us (1.011)
  blocking collectives: 71.7 us -> 59 us
  starting transfers between devices: 5.97 us -> 15.8 us
  waiting for transfers between devices: 73.1 us -> 76.7 us
    all_gather x1 -> x0, blocking collectives: 12 us -> none  [per_device(): column_rows = lax.all_gather(own_rows, 'dp', axis=0, tiled=True)]
    ppermute x0 -> x3, starting transfers between devices: none -> 9.79 us  [the longest x2 6.14 us: keep_up_copies_now(): lax.ppermute(n_now[-1] if n_now else shard_in, net_axis, ledger)]
    ppermute x0 -> x3, waiting for transfers between devices: none -> 4.2 us  [the longest x2 4.2 us: keep_up_copies_now(): lax.ppermute(n_now[-1] if n_now else shard_in, net_axis, ledger)]
  transfers between devices with their start and end apart: 2 -> 5, of which waited for: 2 -> 3; matrix products, arithmetic and copies ran while one was open for 1% -> 2% of each run, Pallas kernels for 0% -> 0%
where the time goes in v1:
time: 185 us; the launch traced here: 184 us
  waiting for transfers between devices  76.7 us (41%)
  blocking collectives  59 us (32%)
  starting transfers between devices  15.8 us (9%)
  between operations  14.2 us (8%)
  local copies, waits for them, and re-layouts  10.8 us (6%)
  matrix products  4.2 us (2%)
  other arithmetic  3.35 us (2%)
    all_to_all x1, blocking collectives, per_device(): lax.all_to_all(send_block, 'ep', split_axis=0, concat_axis=0, tiled=True)  48.6 us
    unnamed x2, waiting for transfers between devices  41.4 us
    all_to_all x1, waiting for transfers between devices, per_device(): lax.all_to_all(own_out.reshape(rows.shape[0], rows.shape[1], -1), 'ep', s...  31.1 us
    all_gather x1, blocking collectives, per_device(): column_table = lax.all_gather(route_table, 'dp', axis=0, tiled=True)  10.4 us
    ppermute x2, starting transfers between devices, keep_up_copies_now(): lax.ppermute(n_now[-1] if n_now else shard_in, net_axis, ledger)  6.14 us
    all_to_all x1, starting transfers between devices, per_device(): lax.all_to_all(own_out.reshape(rows.shape[0], rows.shape[1], -1), 'ep', s...  5.93 us
    ppermute x2, waiting for transfers between devices, keep_up_copies_now(): lax.ppermute(n_now[-1] if n_now else shard_in, net_axis, ledger)  4.2 us
  transfers between devices with their start and end apart: 5, of which 3 were waited for; matrix products, arithmetic and copies ran while one was open for 2% of the time, Pallas kernels for 0%

profile of v1, /device:TPU:8, one launch (start us, length us, event | category | flops | bytes accessed | tf_op | source)
XLA Modules:
  0.0 184.2 jit_solution(13150295631261179928)
XLA Ops:
  6.5 0.0 copy-start
  6.5 3.5 %collective-permute-start = (bf16[4,2048]{1,0:T(4,128)(2,1)}, bf16[4,2048]{1,0:T(4,128)(2,1)S(1)}, u32[]{:S(2)}, u32[]{:S(2)}) collective-permute-start(bf16[4,2048]{1,0:T(4,128)(2,1)} %bitcast.40), channel_id=1, source_target_pairs={{0,128},{128,256},{256,384},{384,0},{1,129},{129,257},{257,385},{3... | collective-permute-start | bytes 49160 | tf_op jit(solution)/shard_map/ppermute | solution.py:33
  10.1 3.7 %collective-permute-start.2 = (bf16[4,2048]{1,0:T(4,128)(2,1)}, bf16[4,2048]{1,0:T(4,128)(2,1)S(1)}, u32[]{:S(2)}, u32[]{:S(2)}) collective-permute-start(bf16[4,2048]{1,0:T(4,128)(2,1)} %bitcast.41), channel_id=1, source_target_pairs={{128,0},{256,128},{384,256},{0,384},{129,1},{257,129},{385,257},{1... | collective-permute-start | bytes 49160 | tf_op jit(solution)/shard_map/ppermute | solution.py:35
  13.7 0.8 add_bitcast_fusion
  14.5 10.4 %all-gather = s32[4,4,16]{2,1,0:T(4,128)S(1)} all-gather(s32[1,4,16]{2,1,0:T(4,128)S(1)} %add_bitcast_fusion), channel_id=1, replica_groups=mesh['dp'=4,'ep'=128] {'dp'}, dimensions={0}, use_global_device_ids=true | all-gather | bytes 1280 | tf_op jit(solution)/shard_map/all_gather | solution.py:48
  24.9 0.1 eq.17
  25.0 0.1 fusion.19
  25.1 0.2 reduce_window_sum.11
  25.3 0.2 select_reduce_fusion
  25.5 0.1 mul.37
  25.6 0.0 collective-permute-done
  25.6 2.6 %collective-permute-start.1 = (bf16[4,2048]{1,0:T(4,128)(2,1)S(1)}, bf16[4,2048]{1,0:T(4,128)(2,1)S(1)}, u32[]{:S(2)}, u32[]{:S(2)}) collective-permute-start(bf16[4,2048]{1,0:T(4,128)(2,1)S(1)} %collective-permute-done), channel_id=1, source_target_pairs={{0,128},{128,256},{256,384},{384,0},{1,129},{129,257},{257,385},{3... | collective-permute-start | bytes 49160 | tf_op jit(solution)/shard_map/ppermute | solution.py:33
  28.3 0.0 collective-permute-done.2
  28.3 4.2 %collective-permute-done.1 = bf16[4,2048]{1,0:T(4,128)(2,1)S(1)} collective-permute-done((bf16[4,2048]{1,0:T(4,128)(2,1)S(1)}, bf16[4,2048]{1,0:T(4,128)(2,1)S(1)}, u32[]{:S(2)}, u32[]{:S(2)}) %collective-permute-start.1) | collective-permute-done | bytes 16416 | tf_op jit(solution)/shard_map/ppermute | solution.py:33
  32.5 0.8 pad_maximum_fusion
  33.3 0.6 gather_fusion
  33.9 3.4 %scatter_custom_fusion = bf16[256,2048]{1,0:T(8,128)(2,1)S(1)} fusion(s32[128]{0:T(128)S(1)} %fusion.24, bf16[16,2048]{1,0:T(8,128)(2,1)S(1)} %reshape.157, s32[1024]{0:T(1024)S(1)} %pad_clamp_fusion.1, bf16[]{:T(256)} %constant.48.clone.1), kind=kCustom, calls=%fused_computation.15 | custom fusion | bytes 1048578 | tf_op jit(solution)/shard_map/scatter | solution.py:64
  37.3 0.7 reshape.158
  38.0 48.6 %all_to_all.10 = bf16[128,2,2048]{2,1,0:T(2,128)(2,1)S(1)} all-to-all(bf16[128,2,2048]{2,1,0:T(2,128)(2,1)S(1)} %reshape.158), channel_id=1, replica_groups=mesh['dp'=4,'ep'=128] {'ep'}, dimensions={0} | all-to-all | bytes 2097152 | tf_op jit(solution)/shard_map/all_to_all | solution.py:67
  86.6 0.4 reshape.159
  87.0 1.6 fusion.5
  88.7 0.0 copy-done
  88.7 2.6 %convolution_convert_fusion = bf16[256,2048]{1,0:T(8,128)(2,1)S(1)} fusion(bf16[256,2048]{1,0:T(8,128)(2,1)S(1)} %reshape.159, bf16[1,192,2048]{2,1,0:T(8,128)(2,1)S(1)} %copy-done, bf16[1,2,192,2048]{3,2,1,0:T(8,128)(2,1)} %param.8, f32[256,192]{0,1:T(8,128)S(1)} %fusion.5), kind=kOutput, calls=%fused_computation.4 | convolution fusion | flops 403472384 | bytes 3866624 | tf_op jit(solution)/shard_map/dot_general | solution.py:20
  91.2 1.5 reshape.160
  92.8 5.9 %all-to-all-start.1 = ((bf16[128,2,2048]{2,1,0:T(2,128)(2,1)}), bf16[128,2,2048]{2,1,0:T(2,128)(2,1)S(1)}, u32[]{:S(2)}, u32[]{:S(2)}) async-start(bf16[128,2,2048]{2,1,0:T(2,128)(2,1)} %reshape.160), calls=%async_computation.1 | async-start | bytes 2097152 | tf_op jit(solution)/shard_map/all_to_all | solution.py:70
  98.7 0.0 all-reduce.3.cloned.1.call-start
  98.8 0.2 fusion.21
  98.9 0.1 fusion.20
  99.0 31.1 %all-to-all-done.1 = bf16[128,2,2048]{2,1,0:T(2,128)(2,1)S(1)} async-done(((bf16[128,2,2048]{2,1,0:T(2,128)(2,1)}), bf16[128,2,2048]{2,1,0:T(2,128)(2,1)S(1)}, u32[]{:S(2)}, u32[]{:S(2)}) %all-to-all-start.1) | async-done | bytes 1048608 | tf_op jit(solution)/shard_map/all_to_all | solution.py:70
  130.1 0.4 reshape.161
  130.6 0.9 gather_fusion.1
  131.5 1.1 fusion.1
  132.6 0.0 all-reduce.3.cloned.1.call-update
  132.6 1.3 dynamic-slice
  134.5 41.4 %all-reduce.3.cloned.1.call-done = bf16[16,2048]{1,0:T(8,128)(2,1)} async-done(((bf16[16,2048]{1,0:T(8,128)(2,1)}), bf16[16,2048]{1,0:T(8,128)(2,1)}) %all-reduce.3.cloned.1.call-update) | async-done | bytes 65552
  175.9 1.4 dynamic-slice_bitcast_fusion
  (8 shorter events, 0.1 us)
Async XLA Ops:
  6.5 82.1 %copy-start = (bf16[1,192,2048]{2,1,0:T(8,128)(2,1)S(1)}, bf16[1,192,2048]{2,1,0:T(8,128)(2,1)}, u32[]{:S(2)}) copy-start(bf16[1,192,2048]{2,1,0:T(8,128)(2,1)} %param.9) | copy-start | bytes 2359300
  6.5 19.1 %collective-permute-start = (bf16[4,2048]{1,0:T(4,128)(2,1)}, bf16[4,2048]{1,0:T(4,128)(2,1)S(1)}, u32[]{:S(2)}, u32[]{:S(2)}) collective-permute-start(bf16[4,2048]{1,0:T(4,128)(2,1)} %bitcast.40), channel_id=1, source_target_pairs={{0,128},{128,256},{256,384},{384,0},{1,129},{129,257},{257,385},{3... | collective-permute-start | bytes 49160 | tf_op jit(solution)/shard_map/ppermute | solution.py:33
  10.1 18.2 %collective-permute-start.2 = (bf16[4,2048]{1,0:T(4,128)(2,1)}, bf16[4,2048]{1,0:T(4,128)(2,1)S(1)}, u32[]{:S(2)}, u32[]{:S(2)}) collective-permute-start(bf16[4,2048]{1,0:T(4,128)(2,1)} %bitcast.41), channel_id=1, source_target_pairs={{128,0},{256,128},{384,256},{0,384},{129,1},{257,129},{385,257},{1... | collective-permute-start | bytes 49160 | tf_op jit(solution)/shard_map/ppermute | solution.py:35
  25.6 6.8 %collective-permute-start.1 = (bf16[4,2048]{1,0:T(4,128)(2,1)S(1)}, bf16[4,2048]{1,0:T(4,128)(2,1)S(1)}, u32[]{:S(2)}, u32[]{:S(2)}) collective-permute-start(bf16[4,2048]{1,0:T(4,128)(2,1)S(1)} %collective-permute-done), channel_id=1, source_target_pairs={{0,128},{128,256},{256,384},{384,0},{1,129},{129,257},{257,385},{3... | collective-permute-start | bytes 49160 | tf_op jit(solution)/shard_map/ppermute | solution.py:33
  92.8 37.4 %all-to-all-start.1 = ((bf16[128,2,2048]{2,1,0:T(2,128)(2,1)}), bf16[128,2,2048]{2,1,0:T(2,128)(2,1)S(1)}, u32[]{:S(2)}, u32[]{:S(2)}) async-start(bf16[128,2,2048]{2,1,0:T(2,128)(2,1)} %reshape.160), calls=%async_computation.1 | async-start | bytes 2097152 | tf_op jit(solution)/shard_map/all_to_all | solution.py:70
  98.7 77.2 %all-reduce.3.cloned.1.call-start = ((), (), s32[]{:S(2)}) async-start(), calls=%async_computation.2 | async-start | bytes 131072
Sparse Core Ops, SparseCore 0:
  132.7 43.1 all-reduce.2
